TPU v7x, 32 devices: a whole 2x2x4 slice. The times are simulated.
32 devices in a mesh: grp: 4 (over y, x), word: 8 (over z, core).
Axes of the slice: x: 2, y: 2, z: 4, core: 2. Of those that a mesh axis runs over, the one named last changes fastest.
Arguments:
- descriptors: bfloat16 [262144, 128], P(('grp', 'word'))
- word_ids: int32 [262144], P(('grp', 'word')), may hold values from 0 to 1023, as said below
Outputs:
- centroids: bfloat16 [1024, 128], P('word')
- nearest: float32 [262144], P(('grp', 'word'))
Inputs may be any that keep to these rules, and one draw needn't show every extreme that they name: `word_ids`: the word ids of one device's descriptors lie in a window of 64 consecutive ids, counted modulo 1024; every word id from 0 to 1023 occurs at least once.
All inputs are finite; a program needn't handle non-finite values.
Results may differ from a plain program's by a relative error of at most 0.0015.
Values may be sent and summed in bfloat16 or wider, within the bound.
No kernel may reach another device: no remote copies, remote signals or barrier semaphores. Data moves between devices by JAX's collectives and lax.ppermute only.
A program may use at most 64 MiB of HBM per device.

v0:
```python
import functools

import jax
import jax.numpy as jnp
from jax import lax
from jax.experimental import pallas as pl
from jax.experimental.pallas import tpu as pltpu
from jax.sharding import PartitionSpec as P


K = 1024
SPREAD = 64
HALF = SPREAD // 2
AUX = 16
BOTH = ("grp", "word")
F32 = jnp.float32
I16 = jnp.int16
I32 = jnp.int32
TOP = 32767.0
BF16 = jnp.bfloat16
NT = (((1,), (1,)), ((), ()))
VMEM = pl.BlockSpec(memory_space=pltpu.VMEM)
HBM = pl.BlockSpec(memory_space=pltpu.HBM)
SMALL = pltpu.CompilerParams(vmem_limit_bytes=16 << 20)


def split3(v):
    hi = v.astype(BF16)
    rest = v - hi.astype(F32)
    mid = rest.astype(BF16)
    low = (rest - mid.astype(F32)).astype(BF16)
    return hi, mid, low


def half_of(groups, words):
    group, word = lax.axis_index("grp"), lax.axis_index("word")
    return (word + word // (words // 2) + group // (groups // 2)) % 2


def sums_kernel(ids_hbm, x_hbm, keep_ref, send_ref, x_ref, ids_ref, sem):
    half = half_of(lax.axis_size("grp"), lax.axis_size("word"))
    load_ids = pltpu.make_async_copy(ids_hbm, ids_ref, sem.at[0])
    load_ids.start()
    load = pltpu.make_async_copy(x_hbm, x_ref, sem.at[1])
    load.start()
    load_ids.wait()
    slot = lax.broadcasted_iota(I32, (SPREAD, 128), 0)
    ids = ids_ref[...]
    at = jnp.bitwise_and(ids, SPREAD - 1)
    total = jnp.zeros((SPREAD, 128), F32)
    pieces = []
    for r in range(ids.shape[0]):
        hit = jnp.where(slot == at[r : r + 1, :], 1.0, 0.0)
        total = total + hit
        pieces.append(hit.astype(BF16))
    first = ids[0:1, 0:1]
    rel = jnp.bitwise_and(ids - first + K // 2, K - 1)
    low = jnp.min(jnp.min(rel, axis=0, keepdims=True), axis=1, keepdims=True)
    start = jnp.bitwise_and(first + low - K // 2, K - 1)
    lane = lax.broadcasted_iota(I32, (AUX, 128), 1)
    line = lax.broadcasted_iota(I32, (AUX, 128), 0)
    own = jnp.bitwise_and(lane, SPREAD - 1)
    word = jnp.bitwise_and(start + jnp.bitwise_and(own - start, SPREAD - 1), K - 1)
    place = ((word // SPREAD) * HALF + jnp.bitwise_and(word, HALF - 1)).astype(F32)
    count = jnp.broadcast_to(jnp.sum(total, axis=1, keepdims=True), (SPREAD, 128))
    load.wait()
    sums = jnp.dot(jnp.concatenate(pieces, axis=1), x_ref[...], preferred_element_type=F32)
    largest = jnp.maximum(jnp.max(jnp.abs(sums), axis=1, keepdims=True), 2.0**-110)
    power = jnp.broadcast_to(jnp.floor(jnp.log2(largest)) - 14.0, (SPREAD, 128))
    rows = jnp.concatenate([count, power], axis=0).T
    stretch = rows[0:AUX, :]
    aux0 = jnp.where(line == 0, jnp.where(lane < HALF, place, pltpu.roll(stretch, HALF, 1)), pltpu.roll(stretch, SPREAD, 1))
    aux1 = jnp.where(line == 0, jnp.where(lane < HALF, pltpu.roll(place, 96, 1), stretch), pltpu.roll(stretch, HALF, 1))
    inside = jnp.logical_and(lane < SPREAD, line < 2)
    aux0 = jnp.where(inside, aux0, 0.0)
    aux1 = jnp.where(inside, aux1, 0.0)
    shift = jnp.exp2(-power).astype(BF16).astype(F32)
    code = jnp.clip(jnp.round(sums * shift), -TOP, TOP)
    keep = jnp.where(half == 0, code[0:HALF], code[HALF:SPREAD])
    send = jnp.where(half == 0, code[HALF:SPREAD], code[0:HALF])
    keep_ref[0:HALF, :] = keep.astype(I32).astype(I16)
    send_ref[0:HALF, :] = send.astype(I32).astype(I16)
    keep_ref[HALF : HALF + AUX, :] = jnp.where(half == 0, aux0, aux1).astype(I32).astype(I16)
    send_ref[HALF : HALF + AUX, :] = pltpu.roll(jnp.where(half == 0, aux1, aux0), SPREAD, 1).astype(I32).astype(I16)


def window_sums(ids, x):
    rows, depth = x.shape
    out = jax.ShapeDtypeStruct((HALF + AUX, depth), I16)
    return pl.pallas_call(
        sums_kernel,
        in_specs=[HBM, HBM],
        out_specs=(VMEM, VMEM, VMEM),
        out_shape=(out, out, jax.ShapeDtypeStruct(x.shape, x.dtype)),
        scratch_shapes=[pltpu.VMEM((rows // 128, 128), I32), pltpu.SemaphoreType.DMA((2,))],
        compiler_params=SMALL,
        name="window_sums",
    )(pltpu.with_memory_space_constraint(ids, pltpu.HBM), pltpu.with_memory_space_constraint(x, pltpu.HBM))


def norms_kernel(x_ref, out_ref):
    n = x_ref.shape[0]
    xf = x_ref[...].astype(F32)
    sq = xf * xf
    hi = sq.astype(BF16)
    low = (sq - hi.astype(F32)).astype(BF16)
    both = jnp.concatenate([hi, low], axis=1)
    ones = jnp.ones((8, both.shape[1]), BF16)
    row = lax.dot_general(ones, both, NT, preferred_element_type=F32)
    for r in range(n // 128):
        out_ref[r : r + 1, :] = row[0:1, r * 128 : (r + 1) * 128]


def norms(x):
    rows, depth = x.shape
    chunk = min(2048, rows)
    return pl.pallas_call(
        norms_kernel,
        grid=(rows // chunk,),
        in_specs=[pl.BlockSpec((chunk, depth), lambda i: (i, 0))],
        out_specs=pl.BlockSpec((chunk // 128, 128), lambda i: (i, 0)),
        out_shape=jax.ShapeDtypeStruct((rows // 128, 128), F32),
        cost_estimate=pl.CostEstimate(flops=2 * rows * depth, bytes_accessed=2 * rows * depth, transcendentals=0),
        compiler_params=SMALL,
        name="norms",
    )(x)


def means_kernel(parts, *refs):
    ins, table_ref = refs[:parts], refs[parts]
    rows = ins[0].shape[0] - AUX
    half = table_ref.shape[0]
    depth = ins[0].shape[1]
    target = lax.broadcasted_iota(I32, (half, 128), 0).astype(F32)
    lane = lax.broadcasted_iota(I32, (1, 128), 1)
    pieces, values = [], []
    count = jnp.zeros((half, 128), F32)
    for ref in ins:
        aux = ref[rows : rows + AUX, :].astype(I32).astype(F32)
        for pair in range(rows // 128):
            a, ea, b, eb = [aux[4 * pair + i : 4 * pair + i + 1, :] for i in range(4)]
            a32, b32 = pltpu.roll(a, 96, 1), pltpu.roll(b, 32, 1)
            place_a = jnp.where(lane < 32, a, a32)
            count_a = jnp.where(lane < 32, a32, pltpu.roll(a, 64, 1))
            power_a = jnp.where(lane < 32, ea, pltpu.roll(ea, 96, 1))
            place_b = jnp.where(lane < 96, pltpu.roll(b, 64, 1), b32)
            count_b = jnp.where(lane < 96, b32, b)
            power_b = jnp.where(lane < 96, pltpu.roll(eb, 64, 1), pltpu.roll(eb, 32, 1))
            place = jnp.where(lane < 64, place_a, place_b)
            amount = jnp.where(lane < 64, count_a, count_b)
            scale = jnp.exp2(jnp.where(lane < 64, power_a, power_b))
            hit = target == place
            count = count + jnp.where(hit, amount, 0.0)
            pieces.append(jnp.where(hit, scale, 0.0).astype(BF16))
            code = ref[128 * pair : 128 * pair + 128, :].astype(I32)
            high = jnp.bitwise_and(code + 128, -256)
            values.append(jnp.concatenate([high.astype(F32).astype(BF16), (code - high).astype(F32).astype(BF16)], axis=1))
    onehot = jnp.concatenate(pieces, axis=1)
    wide = jnp.dot(onehot, jnp.concatenate(values, axis=0), preferred_element_type=F32)
    sums = wide[:, 0:depth] + wide[:, depth : 2 * depth]
    cent = (sums / jnp.sum(count, axis=1, keepdims=True)).astype(BF16)
    write_table(cent, table_ref)


def write_table(cent, table_ref):
    words, depth = cent.shape
    cf = cent.astype(F32)
    norm = jnp.broadcast_to(-0.5 * jnp.sum(cf * cf, axis=1, keepdims=True), (words, depth))
    lane = lax.broadcasted_iota(I32, (words, depth), 1)
    hi, mid, low = [p.astype(F32) for p in split3(norm)]
    extra = jnp.where(lane == 0, hi, jnp.where(lane == 1, mid, jnp.where(lane == 2, low, 0.0)))
    table_ref[:, 0:depth] = cent
    table_ref[:, depth : 2 * depth] = extra.astype(BF16)


def table_kernel(cent_ref, table_ref):
    write_table(cent_ref[...], table_ref)


def tables(cent):
    words, depth = cent.shape
    return pl.pallas_call(
        table_kernel,
        in_specs=[VMEM],
        out_specs=VMEM,
        out_shape=jax.ShapeDtypeStruct((words, 2 * depth), BF16),
        compiler_params=SMALL,
        name="tables",
    )(cent)


def means(parts, half):
    depth = parts[0].shape[1]
    return pl.pallas_call(
        functools.partial(means_kernel, len(parts)),
        in_specs=[VMEM] * len(parts),
        out_specs=VMEM,
        compiler_params=SMALL,
        out_shape=jax.ShapeDtypeStruct((half, 2 * depth), BF16),
        name="means",
    )(*parts)


def own_words(mine_ref, other_ref, own_ref):
    index = lax.axis_index("word")
    even = half_of(lax.axis_size("grp"), lax.axis_size("word")) == 0
    blocks = own_ref.shape[0] // SPREAD
    for b in range(blocks):
        at = (index * blocks + b) % (mine_ref.shape[0] // HALF)
        rows = pl.ds(pl.multiple_of(at * HALF, HALF), HALF)
        mine, other = mine_ref[rows, 0 : own_ref.shape[1]], other_ref[rows, 0 : own_ref.shape[1]]
        own_ref[b * SPREAD : b * SPREAD + HALF, :] = jnp.where(even, mine, other)
        own_ref[b * SPREAD + HALF : (b + 1) * SPREAD, :] = jnp.where(even, other, mine)


def largest(table_ref, x_ref, out_ref, begin, end):
    words = table_ref.shape[0]
    depth = x_ref.shape[1]
    cols = 256
    ones = jnp.ones((cols, depth), BF16)
    for t in range(begin // cols, end // cols):
        full = jnp.concatenate([x_ref[t * cols : (t + 1) * cols, :], ones], axis=1)
        d = lax.dot_general(table_ref[...], full, NT, preferred_element_type=F32)
        row = jnp.max(jnp.max(d.reshape(words // 8, 8, cols), axis=0), axis=0, keepdims=True)
        for r in range(cols // 128):
            at = t * (cols // 128) + r
            out_ref[at : at + 1, :] = row[0:1, r * 128 : (r + 1) * 128]


def first_kernel(table_ref, x_ref, out_ref):
    largest(table_ref, x_ref, out_ref, 0, x_ref.shape[0])


def last_kernel(table_ref, x_ref, mine_ref, near_ref, norm_ref, own_hbm, out_hbm, own_ref, out_ref, sem):
    n, depth = x_ref.shape
    own_words(mine_ref, table_ref, own_ref)
    copies = [pltpu.make_async_copy(own_ref, own_hbm, sem.at[0])]
    copies[0].start()
    bounds = [0, n * 3 // 4, n]
    for i in range(2):
        begin, end = bounds[i], bounds[i + 1]
        largest(table_ref, x_ref, out_ref, begin, end)
        part = slice(begin // 128, end // 128)
        best = jnp.maximum(out_ref[part, :], near_ref[part, :])
        out_ref[part, :] = (norm_ref[part, :] - 2.0 * best) * (1.0 / depth)
        copies.append(pltpu.make_async_copy(out_ref.at[part, :], out_hbm.at[part, :], sem.at[i + 1]))
        copies[-1].start()
    for copy in copies:
        copy.wait()


def nearest_first(table, x):
    rows, depth = x.shape
    words = table.shape[0]
    return pl.pallas_call(
        first_kernel,
        in_specs=[VMEM, VMEM],
        out_specs=VMEM,
        out_shape=jax.ShapeDtypeStruct((rows // 128, 128), F32),
        cost_estimate=pl.CostEstimate(flops=4 * rows * depth * words, bytes_accessed=2 * rows * depth, transcendentals=0),
        compiler_params=SMALL,
        name="nearest_first",
    )(table, x)


def nearest_last(table, x, mine, near, norm, owned):
    rows, depth = x.shape
    words = table.shape[0]
    out, own = (rows // 128, 128), (owned, depth)
    return pl.pallas_call(
        last_kernel,
        in_specs=[VMEM] * 5,
        out_specs=(HBM, HBM),
        out_shape=(jax.ShapeDtypeStruct(own, BF16), jax.ShapeDtypeStruct(out, F32)),
        scratch_shapes=[pltpu.VMEM(own, BF16), pltpu.VMEM(out, F32), pltpu.SemaphoreType.DMA((3,))],
        cost_estimate=pl.CostEstimate(flops=4 * rows * depth * words, bytes_accessed=2 * rows * depth, transcendentals=0),
        compiler_params=SMALL,
        name="nearest_last",
    )(table, x, mine, near, norm)


def moved(a, groups, words, group=0, chip=0, core=0):
    core ^= group // (groups // 2) ^ chip // (words // 4)
    pairs = [(g * words + w, (g ^ group) * words + (w ^ (2 * chip + core))) for g in range(groups) for w in range(words)]
    return lax.ppermute(a, BOTH, pairs)


def chip_order(words):
    chips = words // 2
    return list(range(chips // 2, chips)) + list(range(1, chips // 2))


def group_order(groups):
    return list(range(groups - 1, 0, -1))


def gathered(groups, words, descriptors, word_ids):
    rows, depth = descriptors.shape
    ids = word_ids.reshape(rows // 128, 128)
    keep, send, x = window_sums(ids, descriptors)
    got = moved(send, groups, words, core=1)
    mine = jnp.concatenate([keep[:HALF], got[:HALF], keep[HALF:] + got[HALF:]], axis=0)
    line = [mine] + [moved(mine, groups, words, chip=k) for k in chip_order(words)]
    aux = [a[SPREAD : SPREAD + 2] for a in line]
    aux.append(jnp.zeros((-2 * len(line) % AUX, depth), I16))
    block = jnp.concatenate([a[:SPREAD] for a in line] + aux, axis=0)
    blocks = [block] + [moved(block, groups, words, group=k) for k in group_order(groups)]
    xnorm = norms(x)
    half = means(blocks, K // 2)
    other = moved(half, groups, words, core=1)
    near = nearest_first(half, x)
    cent, near = nearest_last(other, x, half, near, xnorm, K // words)
    return cent, near.reshape(rows)


def summed(words, descriptors, word_ids):
    rows, depth = descriptors.shape
    keep, send, x = window_sums(word_ids.reshape(rows // 128, 128), descriptors)
    index = lax.axis_index("word")
    even = half_of(lax.axis_size("grp"), lax.axis_size("word")) == 0
    near_half = jnp.where(even, keep, send)
    far_half = jnp.where(even, send, keep)
    target = lax.broadcasted_iota(I32, (K // 2, HALF), 0)
    totals, counts = [], []
    for part in (near_half, far_half):
        aux = (part[HALF : HALF + 2, :SPREAD] + part[HALF : HALF + 2, SPREAD:]).astype(I32)
        hit = target == aux[0:1, :HALF]
        counts.append(jnp.sum(jnp.where(hit, aux[0:1, HALF:].astype(F32), 0.0), axis=1))
        scale = jnp.exp2(aux[1, :HALF].astype(F32)).astype(BF16).astype(F32)
        totals.append(jnp.dot(hit.astype(F32), part[:HALF].astype(F32) * scale[:, None], precision=lax.Precision.HIGHEST))
    total, count = lax.psum((jnp.concatenate(totals), jnp.concatenate(counts)), BOTH)
    cent = (total / count[:, None]).astype(BF16)
    table = tables(cent)
    near = nearest_first(table[: K // 2], x)
    _, near = nearest_last(table[K // 2 :], x, table[: K // 2], near, norms(x), SPREAD)
    cent = cent.reshape(2, K // SPREAD, HALF, depth).swapaxes(0, 1).reshape(K, depth)
    owned = K // words
    return lax.dynamic_slice_in_dim(cent, index * owned, owned, 0), near.reshape(rows)


def solution(mesh):
    groups, words = mesh.shape["grp"], mesh.shape["word"]
    small = groups * words * SPREAD <= 2 * K and K // words >= SPREAD
    specs = dict(mesh=mesh, in_specs=(P(BOTH, None), P(BOTH)), out_specs=(P("word", None), P(BOTH)), check_vma=False)
    if not small:
        return jax.shard_map(functools.partial(summed, words), **specs)

    def step(descriptors, word_ids):
        return gathered(groups, words, descriptors, word_ids)

    return jax.shard_map(step, **specs)
```

profile of v0, /device:TPU:0, one launch (start us, length us, event | category | flops | bytes accessed | tf_op | source)
XLA Modules:
  0.0 29.8 jit_solution(3158020204057473458)
XLA Ops:
  0.6 2.4 %window_sums.1 = (s16[48,128]{1,0:T(8,128)(2,1)S(1)}, s16[48,128]{1,0:T(8,128)(2,1)S(1)}, bf16[8192,128]{1,0:T(8,128)(2,1)S(1)}) custom-call(s32[64,128]{1,0:T(8,128)} %bitcast.2, bf16[8192,128]{1,0:T(8,128)(2,1)} %x_hbm.1), custom_call_target="tpu_custom_call" | custom-call | tf_op jit(solution)/shard_map/window_sums/pallas_call | solution.py:90
  3.0 0.6 %collective-permute-start = (s16[48,128]{1,0:T(8,128)(2,1)S(1)}, s16[48,128]{1,0:T(8,128)(2,1)S(1)}, u32[]{:S(2)}, u32[]{:S(2)}) collective-permute-start(s16[48,128]{1,0:T(8,128)(2,1)S(1)} %get-tuple-element.8), channel_id=1, source_target_pairs={{0,1},{1,0},{2,3},{3,2},{4,5},{5,4},{6,7},{7,6},{8,9},{9,8},{10,11... | collective-permute-start | bytes 36872 | tf_op jit(solution)/shard_map/ppermute | solution.py:285
  3.6 0.8 %collective-permute-done = s16[48,128]{1,0:T(8,128)(2,1)S(1)} collective-permute-done((s16[48,128]{1,0:T(8,128)(2,1)S(1)}, s16[48,128]{1,0:T(8,128)(2,1)S(1)}, u32[]{:S(2)}, u32[]{:S(2)}) %collective-permute-start) | collective-permute-done | bytes 12320 | tf_op jit(solution)/shard_map/ppermute | solution.py:285
  4.4 3.0 %collective-permute-start.3 = (s16[80,128]{1,0:T(8,128)(2,1)S(1)}, s16[80,128]{1,0:T(8,128)(2,1)S(1)}, u32[]{:S(2)}, u32[]{:S(2)}) collective-permute-start(s16[80,128]{1,0:T(8,128)(2,1)S(1)} %pad_add_fusion), channel_id=1, source_target_pairs={{0,2},{1,3},{2,0},{3,1},{4,6},{5,7},{6,4},{7,5},{8,10},{9,11},{10,... | collective-permute-start | bytes 61448 | tf_op jit(solution)/shard_map/ppermute | solution.py:285
  7.4 2.0 %collective-permute-start.2 = (s16[80,128]{1,0:T(8,128)(2,1)S(1)}, s16[80,128]{1,0:T(8,128)(2,1)S(1)}, u32[]{:S(2)}, u32[]{:S(2)}) collective-permute-start(s16[80,128]{1,0:T(8,128)(2,1)S(1)} %pad_add_fusion), channel_id=1, source_target_pairs={{0,7},{1,6},{2,5},{3,4},{4,3},{5,2},{6,1},{7,0},{8,15},{9,14},{10,... | collective-permute-start | bytes 61448 | tf_op jit(solution)/shard_map/ppermute | solution.py:285
  9.3 0.1 collective-permute-start.1
  9.5 0.0 collective-permute-done.3
  9.5 3.1 %collective-permute-done.2 = s16[80,128]{1,0:T(8,128)(2,1)S(1)} collective-permute-done((s16[80,128]{1,0:T(8,128)(2,1)S(1)}, s16[80,128]{1,0:T(8,128)(2,1)S(1)}, u32[]{:S(2)}, u32[]{:S(2)}) %collective-permute-start.2) | collective-permute-done | bytes 20512 | tf_op jit(solution)/shard_map/ppermute | solution.py:285
  12.5 1.1 %collective-permute-done.1 = s16[80,128]{1,0:T(8,128)(2,1)S(1)} collective-permute-done((s16[80,128]{1,0:T(8,128)(2,1)S(1)}, s16[80,128]{1,0:T(8,128)(2,1)S(1)}, u32[]{:S(2)}, u32[]{:S(2)}) %collective-permute-start.1) | collective-permute-done | bytes 20512 | tf_op jit(solution)/shard_map/ppermute | solution.py:285
  13.7 0.1 concatenate.9.refs_0_
  13.8 1.5 %collective-permute-start.6 = (s16[272,128]{1,0:T(8,128)(2,1)S(1)}, s16[272,128]{1,0:T(8,128)(2,1)S(1)}, u32[]{:S(2)}, u32[]{:S(2)}) collective-permute-start(s16[272,128]{1,0:T(8,128)(2,1)S(1)} %concatenate.9.refs_0_), channel_id=1, source_target_pairs={{0,8},{1,9},{2,10},{3,11},{4,12},{5,13},{6,14},{7,15},{8,0},{9,1},... | collective-permute-start | bytes 208904 | tf_op jit(solution)/shard_map/ppermute | solution.py:285
  15.3 1.5 %collective-permute-start.5 = (s16[272,128]{1,0:T(8,128)(2,1)S(1)}, s16[272,128]{1,0:T(8,128)(2,1)S(1)}, u32[]{:S(2)}, u32[]{:S(2)}) collective-permute-start(s16[272,128]{1,0:T(8,128)(2,1)S(1)} %concatenate.9.refs_0_), channel_id=1, source_target_pairs={{0,17},{1,16},{2,19},{3,18},{4,21},{5,20},{6,23},{7,22},{8,25},{9,... | collective-permute-start | bytes 208904 | tf_op jit(solution)/shard_map/ppermute | solution.py:285
  16.8 0.2 collective-permute-start.4
  17.1 1.5 %collective-permute-done.6.refs_3_ = s16[272,128]{1,0:T(8,128)(2,1)S(1)} collective-permute-done((s16[272,128]{1,0:T(8,128)(2,1)S(1)}, s16[272,128]{1,0:T(8,128)(2,1)S(1)}, u32[]{:S(2)}, u32[]{:S(2)}) %collective-permute-start.6) | collective-permute-done | bytes 69664 | tf_op jit(solution)/shard_map/ppermute | solution.py:285
  18.6 0.7 %collective-permute-done.5.refs_2_ = s16[272,128]{1,0:T(8,128)(2,1)S(1)} collective-permute-done((s16[272,128]{1,0:T(8,128)(2,1)S(1)}, s16[272,128]{1,0:T(8,128)(2,1)S(1)}, u32[]{:S(2)}, u32[]{:S(2)}) %collective-permute-start.5) | collective-permute-done | bytes 69664 | tf_op jit(solution)/shard_map/ppermute | solution.py:285
  19.3 2.6 %collective-permute-done.4.refs_1_ = s16[272,128]{1,0:T(8,128)(2,1)S(1)} collective-permute-done((s16[272,128]{1,0:T(8,128)(2,1)S(1)}, s16[272,128]{1,0:T(8,128)(2,1)S(1)}, u32[]{:S(2)}, u32[]{:S(2)}) %collective-permute-start.4) | collective-permute-done | bytes 69664 | tf_op jit(solution)/shard_map/ppermute | solution.py:285
  21.8 0.8 %means.1.table_ref.mine_ref = bf16[512,256]{1,0:T(8,128)(2,1)S(1)} custom-call(s16[272,128]{1,0:T(8,128)(2,1)S(1)} %concatenate.9.refs_0_, s16[272,128]{1,0:T(8,128)(2,1)S(1)} %collective-permute-done.4.refs_1_, s16[272,128]{1,0:T(8,128)(2,1)S(1)} %collective-permute-done.5.refs_2_, s16[272,128]{1,0:T(8,128)(2,1)S(1)} %collective-permute-done.6.refs_3_), custom_call_target="tpu_custom_call" | custom-call | tf_op jit(solution)/shard_map/means/pallas_call | solution.py:194
  22.6 0.2 collective-permute-start.7
  22.8 1.6 %norms.1.norm_ref = f32[64,128]{1,0:T(8,128)S(1)} custom-call(bf16[8192,128]{1,0:T(8,128)(2,1)S(1)} %get-tuple-element.9.x_ref), custom_call_target="tpu_custom_call" | custom-call | flops 2097152 | bytes 2097152 | tf_op jit(solution)/shard_map/norms/pallas_call | solution.py:117
  24.4 2.4 %nearest_first.1.near_ref = f32[64,128]{1,0:T(8,128)S(1)} custom-call(bf16[512,256]{1,0:T(8,128)(2,1)S(1)} %means.1.table_ref.mine_ref, bf16[8192,128]{1,0:T(8,128)(2,1)S(1)} %get-tuple-element.9.x_ref), custom_call_target="tpu_custom_call" | custom-call | flops 2147483648 | bytes 2097152 | tf_op jit(solution)/shard_map/nearest_first/pallas_call | solution.py:255
  26.8 0.0 collective-permute-done.7.table_ref
  26.8 3.0 %nearest_last.1 = (bf16[128,128]{1,0:T(8,128)(2,1)}, f32[64,128]{1,0:T(8,128)}) custom-call(bf16[512,256]{1,0:T(8,128)(2,1)S(1)} %collective-permute-done.7.table_ref, bf16[8192,128]{1,0:T(8,128)(2,1)S(1)} %get-tuple-element.9.x_ref, bf16[512,256]{1,0:T(8,128)(2,1)S(1)} %means.1.table_ref.mine_ref, f32[64,128]{1,0:T(8,128)S(1)} %nearest_first.1.near_ref, ...), custom_call_target="tpu_custom_call" | custom-call | flops 2147483648 | bytes 2097152 | tf_op jit(solution)/shard_map/nearest_last/pallas_call | solution.py:270
  (12 shorter events, 0.0 us)
Async XLA Ops:
  3.0 1.4 %collective-permute-start = (s16[48,128]{1,0:T(8,128)(2,1)S(1)}, s16[48,128]{1,0:T(8,128)(2,1)S(1)}, u32[]{:S(2)}, u32[]{:S(2)}) collective-permute-start(s16[48,128]{1,0:T(8,128)(2,1)S(1)} %get-tuple-element.8), channel_id=1, source_target_pairs={{0,1},{1,0},{2,3},{3,2},{4,5},{5,4},{6,7},{7,6},{8,9},{9,8},{10,11... | collective-permute-start | bytes 36872 | tf_op jit(solution)/shard_map/ppermute | solution.py:285
  4.4 5.1 %collective-permute-start.3 = (s16[80,128]{1,0:T(8,128)(2,1)S(1)}, s16[80,128]{1,0:T(8,128)(2,1)S(1)}, u32[]{:S(2)}, u32[]{:S(2)}) collective-permute-start(s16[80,128]{1,0:T(8,128)(2,1)S(1)} %pad_add_fusion), channel_id=1, source_target_pairs={{0,2},{1,3},{2,0},{3,1},{4,6},{5,7},{6,4},{7,5},{8,10},{9,11},{10,... | collective-permute-start | bytes 61448 | tf_op jit(solution)/shard_map/ppermute | solution.py:285
  7.4 5.2 %collective-permute-start.2 = (s16[80,128]{1,0:T(8,128)(2,1)S(1)}, s16[80,128]{1,0:T(8,128)(2,1)S(1)}, u32[]{:S(2)}, u32[]{:S(2)}) collective-permute-start(s16[80,128]{1,0:T(8,128)(2,1)S(1)} %pad_add_fusion), channel_id=1, source_target_pairs={{0,7},{1,6},{2,5},{3,4},{4,3},{5,2},{6,1},{7,0},{8,15},{9,14},{10,... | collective-permute-start | bytes 61448 | tf_op jit(solution)/shard_map/ppermute | solution.py:285
  9.3 4.3 %collective-permute-start.1 = (s16[80,128]{1,0:T(8,128)(2,1)S(1)}, s16[80,128]{1,0:T(8,128)(2,1)S(1)}, u32[]{:S(2)}, u32[]{:S(2)}) collective-permute-start(s16[80,128]{1,0:T(8,128)(2,1)S(1)} %pad_add_fusion), channel_id=1, source_target_pairs={{0,5},{1,4},{2,7},{3,6},{4,1},{5,0},{6,3},{7,2},{8,13},{9,12},{10,... | collective-permute-start | bytes 61448 | tf_op jit(solution)/shard_map/ppermute | solution.py:285
  13.8 4.8 %collective-permute-start.6 = (s16[272,128]{1,0:T(8,128)(2,1)S(1)}, s16[272,128]{1,0:T(8,128)(2,1)S(1)}, u32[]{:S(2)}, u32[]{:S(2)}) collective-permute-start(s16[272,128]{1,0:T(8,128)(2,1)S(1)} %concatenate.9.refs_0_), channel_id=1, source_target_pairs={{0,8},{1,9},{2,10},{3,11},{4,12},{5,13},{6,14},{7,15},{8,0},{9,1},... | collective-permute-start | bytes 208904 | tf_op jit(solution)/shard_map/ppermute | solution.py:285
  15.3 4.0 %collective-permute-start.5 = (s16[272,128]{1,0:T(8,128)(2,1)S(1)}, s16[272,128]{1,0:T(8,128)(2,1)S(1)}, u32[]{:S(2)}, u32[]{:S(2)}) collective-permute-start(s16[272,128]{1,0:T(8,128)(2,1)S(1)} %concatenate.9.refs_0_), channel_id=1, source_target_pairs={{0,17},{1,16},{2,19},{3,18},{4,21},{5,20},{6,23},{7,22},{8,25},{9,... | collective-permute-start | bytes 208904 | tf_op jit(solution)/shard_map/ppermute | solution.py:285
  16.8 5.0 %collective-permute-start.4 = (s16[272,128]{1,0:T(8,128)(2,1)S(1)}, s16[272,128]{1,0:T(8,128)(2,1)S(1)}, u32[]{:S(2)}, u32[]{:S(2)}) collective-permute-start(s16[272,128]{1,0:T(8,128)(2,1)S(1)} %concatenate.9.refs_0_), channel_id=1, source_target_pairs={{0,25},{1,24},{2,27},{3,26},{4,29},{5,28},{6,31},{7,30},{8,17},{9,... | collective-permute-start | bytes 208904 | tf_op jit(solution)/shard_map/ppermute | solution.py:285
  22.6 4.2 %collective-permute-start.7 = (bf16[512,256]{1,0:T(8,128)(2,1)S(1)}, bf16[512,256]{1,0:T(8,128)(2,1)S(1)}, u32[]{:S(2)}, u32[]{:S(2)}) collective-permute-start(bf16[512,256]{1,0:T(8,128)(2,1)S(1)} %means.1.table_ref.mine_ref), channel_id=1, source_target_pairs={{0,1},{1,0},{2,3},{3,2},{4,5},{5,4},{6,7},{7,6},{8,9},{9,8},{10,11... | collective-permute-start | bytes 786440 | tf_op jit(solution)/shard_map/ppermute | solution.py:285
where the time goes:
time: 30 us; the launch traced here: 29.8 us
  Pallas kernels  10.1 us (34%)
  waiting for transfers between devices  9.81 us (33%)
  starting transfers between devices  9.09 us (30%)
  between operations  0.68 us (2%)
    ppermute x8, waiting for transfers between devices, moved(): return lax.ppermute(a, BOTH, pairs)  9.81 us
    ppermute x8, starting transfers between devices, moved(): return lax.ppermute(a, BOTH, pairs)  9.09 us
    pallas_call x1, Pallas kernels, nearest_last(): pl.pallas_call(last_kernel, in_specs=[VMEM] * 5, out_specs=(HBM, HBM), ou...  3.03 us
    pallas_call x1, Pallas kernels, nearest_first(): pl.pallas_call(first_kernel, in_specs=[VMEM, VMEM], out_specs=VMEM, out_s...  2.4 us
    pallas_call x1, Pallas kernels, window_sums(): pl.pallas_call(sums_kernel, in_specs=[HBM, HBM], out_specs=(VMEM, VMEM, V...  2.36 us
    pallas_call x1, Pallas kernels, norms(): pl.pallas_call(norms_kernel, grid=(rows // chunk,), in_specs=[pl.BlockSpe...  1.56 us
    pallas_call x1, Pallas kernels, means(): pl.pallas_call(functools.partial(means_kernel, len(parts)), in_specs=[VME...  0.76 us
  transfers between devices with their start and end apart: 8, of which 6 were waited for; matrix products, arithmetic and copies ran while one was open for 0% of the time, Pallas kernels for 13%

commit v1 on v0

--- a/solution.py
+++ b/solution.py
@@ -32,9 +32,13 @@
     return hi, mid, low
 
 
+def bits(number, size):
+    return sum((number // (1 << b)) % 2 for b in range(size.bit_length()))
+
+
 def half_of(groups, words):
     group, word = lax.axis_index("grp"), lax.axis_index("word")
-    return (word + word // (words // 2) + group // (groups // 2)) % 2
+    return (word + bits(word // 2, words) + bits(group, groups)) % 2
 
 
 def sums_kernel(ids_hbm, x_hbm, keep_ref, send_ref, x_ref, ids_ref, sem):
@@ -280,14 +284,9 @@
 
 
 def moved(a, groups, words, group=0, chip=0, core=0):
-    core ^= group // (groups // 2) ^ chip // (words // 4)
+    core ^= (bits(group, groups) + bits(chip, words)) % 2
     pairs = [(g * words + w, (g ^ group) * words + (w ^ (2 * chip + core))) for g in range(groups) for w in range(words)]
     return lax.ppermute(a, BOTH, pairs)
-
-
-def chip_order(words):
-    chips = words // 2
-    return list(range(chips // 2, chips)) + list(range(1, chips // 2))
 
 
 def group_order(groups):
@@ -300,7 +299,13 @@
     keep, send, x = window_sums(ids, descriptors)
     got = moved(send, groups, words, core=1)
     mine = jnp.concatenate([keep[:HALF], got[:HALF], keep[HALF:] + got[HALF:]], axis=0)
-    line = [mine] + [moved(mine, groups, words, chip=k) for k in chip_order(words)]
+    lines = mine[None]
+    chip = words // 4
+    while chip:
+        met = moved(lines.reshape(-1, depth), groups, words, chip=chip)
+        lines = jnp.concatenate([lines, met.reshape(lines.shape)], axis=0)
+        chip //= 2
+    line = list(lines)
     aux = [a[SPREAD : SPREAD + 2] for a in line]
     aux.append(jnp.zeros((-2 * len(line) % AUX, depth), I16))
     block = jnp.concatenate([a[:SPREAD] for a in line] + aux, axis=0)

time: 30 us -> 29.6 us (0.987)
  waiting for transfers between devices: 9.81 us -> 9.22 us
    ppermute x8 -> x7, waiting for transfers between devices: 9.81 us -> 9.22 us  [moved(): return lax.ppermute(a, BOTH, pairs)]
    ppermute x8 -> x7, starting transfers between devices: 9.09 us -> 9.25 us  [moved(): return lax.ppermute(a, BOTH, pairs)]
  transfers between devices with their start and end apart: 8 -> 7, of which waited for: 6 -> 6; matrix products, arithmetic and copies ran while one was open for 0% -> 0% of each run, Pallas kernels for 13% -> 14%
where the time goes in v1:
time: 29.6 us; the launch traced here: 29.4 us
  Pallas kernels  10.1 us (34%)
  starting transfers between devices  9.25 us (31%)
  waiting for transfers between devices  9.22 us (31%)
  between operations  0.68 us (2%)
    ppermute x7, starting transfers between devices, moved(): return lax.ppermute(a, BOTH, pairs)  9.25 us
    ppermute x7, waiting for transfers between devices, moved(): return lax.ppermute(a, BOTH, pairs)  9.22 us
    pallas_call x1, Pallas kernels, nearest_last(): pl.pallas_call(last_kernel, in_specs=[VMEM] * 5, out_specs=(HBM, HBM), ou...  3.03 us
    pallas_call x1, Pallas kernels, nearest_first(): pl.pallas_call(first_kernel, in_specs=[VMEM, VMEM], out_specs=VMEM, out_s...  2.4 us
    pallas_call x1, Pallas kernels, window_sums(): pl.pallas_call(sums_kernel, in_specs=[HBM, HBM], out_specs=(VMEM, VMEM, V...  2.36 us
    pallas_call x1, Pallas kernels, norms(): pl.pallas_call(norms_kernel, grid=(rows // chunk,), in_specs=[pl.BlockSpe...  1.58 us
    pallas_call x1, Pallas kernels, means(): pl.pallas_call(functools.partial(means_kernel, len(parts)), in_specs=[VME...  0.76 us
  transfers between devices with their start and end apart: 7, of which 6 were waited for; matrix products, arithmetic and copies ran while one was open for 0% of the time, Pallas kernels for 14%

profile of v1, /device:TPU:0, one launch (start us, length us, event | category | flops | bytes accessed | tf_op | source)
XLA Modules:
  0.0 29.4 jit_solution(10501701767060386911)
XLA Ops:
  0.6 2.4 %window_sums.1 = (s16[48,128]{1,0:T(8,128)(2,1)S(1)}, s16[48,128]{1,0:T(8,128)(2,1)S(1)}, bf16[8192,128]{1,0:T(8,128)(2,1)S(1)}) custom-call(s32[64,128]{1,0:T(8,128)} %bitcast.8, bf16[8192,128]{1,0:T(8,128)(2,1)} %x_hbm.1), custom_call_target="tpu_custom_call" | custom-call | tf_op jit(solution)/shard_map/window_sums/pallas_call | solution.py:94
  3.0 0.6 %collective-permute-start = (s16[48,128]{1,0:T(8,128)(2,1)S(1)}, s16[48,128]{1,0:T(8,128)(2,1)S(1)}, u32[]{:S(2)}, u32[]{:S(2)}) collective-permute-start(s16[48,128]{1,0:T(8,128)(2,1)S(1)} %get-tuple-element.8), channel_id=1, source_target_pairs={{0,1},{1,0},{2,3},{3,2},{4,5},{5,4},{6,7},{7,6},{8,9},{9,8},{10,11... | collective-permute-start | bytes 36872 | tf_op jit(solution)/shard_map/ppermute | solution.py:289
  3.6 0.8 %collective-permute-done = s16[48,128]{1,0:T(8,128)(2,1)S(1)} collective-permute-done((s16[48,128]{1,0:T(8,128)(2,1)S(1)}, s16[48,128]{1,0:T(8,128)(2,1)S(1)}, u32[]{:S(2)}, u32[]{:S(2)}) %collective-permute-start) | collective-permute-done | bytes 12320 | tf_op jit(solution)/shard_map/ppermute | solution.py:289
  4.4 3.8 %collective-permute-start.1 = (s16[80,128]{1,0:T(8,128)(2,1)S(1)}, s16[80,128]{1,0:T(8,128)(2,1)S(1)}, u32[]{:S(2)}, u32[]{:S(2)}) collective-permute-start(s16[80,128]{1,0:T(8,128)(2,1)S(1)} %get-tuple-element.17), channel_id=1, source_target_pairs={{0,5},{1,4},{2,7},{3,6},{4,1},{5,0},{6,3},{7,2},{8,13},{9,12},{10,... | collective-permute-start | bytes 61448 | tf_op jit(solution)/shard_map/ppermute | solution.py:289
  8.2 1.5 %collective-permute-done.1 = s16[80,128]{1,0:T(8,128)(2,1)S(1)} collective-permute-done((s16[80,128]{1,0:T(8,128)(2,1)S(1)}, s16[80,128]{1,0:T(8,128)(2,1)S(1)}, u32[]{:S(2)}, u32[]{:S(2)}) %collective-permute-start.1) | collective-permute-done | bytes 20512 | tf_op jit(solution)/shard_map/ppermute | solution.py:289
  9.6 1.6 %collective-permute-start.2 = (s16[160,128]{1,0:T(8,128)(2,1)S(1)}, s16[160,128]{1,0:T(8,128)(2,1)S(1)}, u32[]{:S(2)}, u32[]{:S(2)}) collective-permute-start(s16[160,128]{1,0:T(8,128)(2,1)S(1)} %bitcast.7), channel_id=1, source_target_pairs={{0,3},{1,2},{2,1},{3,0},{4,7},{5,6},{6,5},{7,4},{8,11},{9,10},{10,... | collective-permute-start | bytes 122888 | tf_op jit(solution)/shard_map/ppermute | solution.py:289
  11.3 1.8 %collective-permute-done.2 = s16[160,128]{1,0:T(8,128)(2,1)S(1)} collective-permute-done((s16[160,128]{1,0:T(8,128)(2,1)S(1)}, s16[160,128]{1,0:T(8,128)(2,1)S(1)}, u32[]{:S(2)}, u32[]{:S(2)}) %collective-permute-start.2) | collective-permute-done | bytes 40992 | tf_op jit(solution)/shard_map/ppermute | solution.py:289
  13.1 0.1 concatenate.13.refs_0_
  13.2 1.7 %collective-permute-start.5 = (s16[272,128]{1,0:T(8,128)(2,1)S(1)}, s16[272,128]{1,0:T(8,128)(2,1)S(1)}, u32[]{:S(2)}, u32[]{:S(2)}) collective-permute-start(s16[272,128]{1,0:T(8,128)(2,1)S(1)} %concatenate.13.refs_0_), channel_id=1, source_target_pairs={{0,9},{1,8},{2,11},{3,10},{4,13},{5,12},{6,15},{7,14},{8,1},{9,0},... | collective-permute-start | bytes 208904 | tf_op jit(solution)/shard_map/ppermute | solution.py:289
  14.9 1.5 %collective-permute-start.4 = (s16[272,128]{1,0:T(8,128)(2,1)S(1)}, s16[272,128]{1,0:T(8,128)(2,1)S(1)}, u32[]{:S(2)}, u32[]{:S(2)}) collective-permute-start(s16[272,128]{1,0:T(8,128)(2,1)S(1)} %concatenate.13.refs_0_), channel_id=1, source_target_pairs={{0,17},{1,16},{2,19},{3,18},{4,21},{5,20},{6,23},{7,22},{8,25},{9,... | collective-permute-start | bytes 208904 | tf_op jit(solution)/shard_map/ppermute | solution.py:289
  16.3 0.1 collective-permute-start.3
  16.5 0.8 %collective-permute-done.5.refs_3_ = s16[272,128]{1,0:T(8,128)(2,1)S(1)} collective-permute-done((s16[272,128]{1,0:T(8,128)(2,1)S(1)}, s16[272,128]{1,0:T(8,128)(2,1)S(1)}, u32[]{:S(2)}, u32[]{:S(2)}) %collective-permute-start.5) | collective-permute-done | bytes 69664 | tf_op jit(solution)/shard_map/ppermute | solution.py:289
  17.3 2.6 %collective-permute-done.4.refs_2_ = s16[272,128]{1,0:T(8,128)(2,1)S(1)} collective-permute-done((s16[272,128]{1,0:T(8,128)(2,1)S(1)}, s16[272,128]{1,0:T(8,128)(2,1)S(1)}, u32[]{:S(2)}, u32[]{:S(2)}) %collective-permute-start.4) | collective-permute-done | bytes 69664 | tf_op jit(solution)/shard_map/ppermute | solution.py:289
  19.9 1.6 %collective-permute-done.3.refs_1_ = s16[272,128]{1,0:T(8,128)(2,1)S(1)} collective-permute-done((s16[272,128]{1,0:T(8,128)(2,1)S(1)}, s16[272,128]{1,0:T(8,128)(2,1)S(1)}, u32[]{:S(2)}, u32[]{:S(2)}) %collective-permute-start.3) | collective-permute-done | bytes 69664 | tf_op jit(solution)/shard_map/ppermute | solution.py:289
  21.6 0.8 %means.1.table_ref.mine_ref = bf16[512,256]{1,0:T(8,128)(2,1)S(1)} custom-call(s16[272,128]{1,0:T(8,128)(2,1)S(1)} %concatenate.13.refs_0_, s16[272,128]{1,0:T(8,128)(2,1)S(1)} %collective-permute-done.3.refs_1_, s16[272,128]{1,0:T(8,128)(2,1)S(1)} %collective-permute-done.4.refs_2_, s16[272,128]{1,0:T(8,128)(2,1)S(1)} %collective-permute-done.5.refs_3_), custom_call_target="tpu_custom_call" | custom-call | tf_op jit(solution)/shard_map/means/pallas_call | solution.py:198
  22.3 0.1 collective-permute-start.6
  22.4 1.6 %norms.1.norm_ref = f32[64,128]{1,0:T(8,128)S(1)} custom-call(bf16[8192,128]{1,0:T(8,128)(2,1)S(1)} %get-tuple-element.9.x_ref), custom_call_target="tpu_custom_call" | custom-call | flops 2097152 | bytes 2097152 | tf_op jit(solution)/shard_map/norms/pallas_call | solution.py:121
  24.0 2.4 %nearest_first.1.near_ref = f32[64,128]{1,0:T(8,128)S(1)} custom-call(bf16[512,256]{1,0:T(8,128)(2,1)S(1)} %means.1.table_ref.mine_ref, bf16[8192,128]{1,0:T(8,128)(2,1)S(1)} %get-tuple-element.9.x_ref), custom_call_target="tpu_custom_call" | custom-call | flops 2147483648 | bytes 2097152 | tf_op jit(solution)/shard_map/nearest_first/pallas_call | solution.py:259
  26.4 0.0 collective-permute-done.6.table_ref
  26.4 3.0 %nearest_last.1 = (bf16[128,128]{1,0:T(8,128)(2,1)}, f32[64,128]{1,0:T(8,128)}) custom-call(bf16[512,256]{1,0:T(8,128)(2,1)S(1)} %collective-permute-done.6.table_ref, bf16[8192,128]{1,0:T(8,128)(2,1)S(1)} %get-tuple-element.9.x_ref, bf16[512,256]{1,0:T(8,128)(2,1)S(1)} %means.1.table_ref.mine_ref, f32[64,128]{1,0:T(8,128)S(1)} %nearest_first.1.near_ref, ...), custom_call_target="tpu_custom_call" | custom-call | flops 2147483648 | bytes 2097152 | tf_op jit(solution)/shard_map/nearest_last/pallas_call | solution.py:274
  (11 shorter events, 0.0 us)
Async XLA Ops:
  3.0 1.4 %collective-permute-start = (s16[48,128]{1,0:T(8,128)(2,1)S(1)}, s16[48,128]{1,0:T(8,128)(2,1)S(1)}, u32[]{:S(2)}, u32[]{:S(2)}) collective-permute-start(s16[48,128]{1,0:T(8,128)(2,1)S(1)} %get-tuple-element.8), channel_id=1, source_target_pairs={{0,1},{1,0},{2,3},{3,2},{4,5},{5,4},{6,7},{7,6},{8,9},{9,8},{10,11... | collective-permute-start | bytes 36872 | tf_op jit(solution)/shard_map/ppermute | solution.py:289
  4.4 5.2 %collective-permute-start.1 = (s16[80,128]{1,0:T(8,128)(2,1)S(1)}, s16[80,128]{1,0:T(8,128)(2,1)S(1)}, u32[]{:S(2)}, u32[]{:S(2)}) collective-permute-start(s16[80,128]{1,0:T(8,128)(2,1)S(1)} %get-tuple-element.17), channel_id=1, source_target_pairs={{0,5},{1,4},{2,7},{3,6},{4,1},{5,0},{6,3},{7,2},{8,13},{9,12},{10,... | collective-permute-start | bytes 61448 | tf_op jit(solution)/shard_map/ppermute | solution.py:289
  9.6 3.4 %collective-permute-start.2 = (s16[160,128]{1,0:T(8,128)(2,1)S(1)}, s16[160,128]{1,0:T(8,128)(2,1)S(1)}, u32[]{:S(2)}, u32[]{:S(2)}) collective-permute-start(s16[160,128]{1,0:T(8,128)(2,1)S(1)} %bitcast.7), channel_id=1, source_target_pairs={{0,3},{1,2},{2,1},{3,0},{4,7},{5,6},{6,5},{7,4},{8,11},{9,10},{10,... | collective-permute-start | bytes 122888 | tf_op jit(solution)/shard_map/ppermute | solution.py:289
  13.2 4.1 %collective-permute-start.5 = (s16[272,128]{1,0:T(8,128)(2,1)S(1)}, s16[272,128]{1,0:T(8,128)(2,1)S(1)}, u32[]{:S(2)}, u32[]{:S(2)}) collective-permute-start(s16[272,128]{1,0:T(8,128)(2,1)S(1)} %concatenate.13.refs_0_), channel_id=1, source_target_pairs={{0,9},{1,8},{2,11},{3,10},{4,13},{5,12},{6,15},{7,14},{8,1},{9,0},... | collective-permute-start | bytes 208904 | tf_op jit(solution)/shard_map/ppermute | solution.py:289
  14.9 5.0 %collective-permute-start.4 = (s16[272,128]{1,0:T(8,128)(2,1)S(1)}, s16[272,128]{1,0:T(8,128)(2,1)S(1)}, u32[]{:S(2)}, u32[]{:S(2)}) collective-permute-start(s16[272,128]{1,0:T(8,128)(2,1)S(1)} %concatenate.13.refs_0_), channel_id=1, source_target_pairs={{0,17},{1,16},{2,19},{3,18},{4,21},{5,20},{6,23},{7,22},{8,25},{9,... | collective-permute-start | bytes 208904 | tf_op jit(solution)/shard_map/ppermute | solution.py:289
  16.3 5.2 %collective-permute-start.3 = (s16[272,128]{1,0:T(8,128)(2,1)S(1)}, s16[272,128]{1,0:T(8,128)(2,1)S(1)}, u32[]{:S(2)}, u32[]{:S(2)}) collective-permute-start(s16[272,128]{1,0:T(8,128)(2,1)S(1)} %concatenate.13.refs_0_), channel_id=1, source_target_pairs={{0,24},{1,25},{2,26},{3,27},{4,28},{5,29},{6,30},{7,31},{8,16},{9,... | collective-permute-start | bytes 208904 | tf_op jit(solution)/shard_map/ppermute | solution.py:289
  22.3 4.1 %collective-permute-start.6 = (bf16[512,256]{1,0:T(8,128)(2,1)S(1)}, bf16[512,256]{1,0:T(8,128)(2,1)S(1)}, u32[]{:S(2)}, u32[]{:S(2)}) collective-permute-start(bf16[512,256]{1,0:T(8,128)(2,1)S(1)} %means.1.table_ref.mine_ref), channel_id=1, source_target_pairs={{0,1},{1,0},{2,3},{3,2},{4,5},{5,4},{6,7},{7,6},{8,9},{9,8},{10,11... | collective-permute-start | bytes 786440 | tf_op jit(solution)/shard_map/ppermute | solution.py:289

commit v2 on v1

--- a/solution.py
+++ b/solution.py
@@ -45,8 +45,10 @@
     half = half_of(lax.axis_size("grp"), lax.axis_size("word"))
     load_ids = pltpu.make_async_copy(ids_hbm, ids_ref, sem.at[0])
     load_ids.start()
-    load = pltpu.make_async_copy(x_hbm, x_ref, sem.at[1])
-    load.start()
+    cuts = (slice(0, x_ref.shape[0] // 2), slice(x_ref.shape[0] // 2, x_ref.shape[0]))
+    loads = [pltpu.make_async_copy(x_hbm.at[c, :], x_ref.at[c, :], sem.at[1 + i]) for i, c in enumerate(cuts)]
+    for load in loads:
+        load.start()
     load_ids.wait()
     slot = lax.broadcasted_iota(I32, (SPREAD, 128), 0)
     ids = ids_ref[...]
@@ -67,8 +69,11 @@
     word = jnp.bitwise_and(start + jnp.bitwise_and(own - start, SPREAD - 1), K - 1)
     place = ((word // SPREAD) * HALF + jnp.bitwise_and(word, HALF - 1)).astype(F32)
     count = jnp.broadcast_to(jnp.sum(total, axis=1, keepdims=True), (SPREAD, 128))
-    load.wait()
-    sums = jnp.dot(jnp.concatenate(pieces, axis=1), x_ref[...], preferred_element_type=F32)
+    onehot = jnp.concatenate(pieces, axis=1)
+    sums = jnp.zeros((SPREAD, x_ref.shape[1]), F32)
+    for load, c in zip(loads, cuts):
+        load.wait()
+        sums = sums + jnp.dot(onehot[:, c], x_ref[c, :], preferred_element_type=F32)
     largest = jnp.maximum(jnp.max(jnp.abs(sums), axis=1, keepdims=True), 2.0**-110)
     power = jnp.broadcast_to(jnp.floor(jnp.log2(largest)) - 14.0, (SPREAD, 128))
     rows = jnp.concatenate([count, power], axis=0).T
@@ -96,7 +101,7 @@
         in_specs=[HBM, HBM],
         out_specs=(VMEM, VMEM, VMEM),
         out_shape=(out, out, jax.ShapeDtypeStruct(x.shape, x.dtype)),
-        scratch_shapes=[pltpu.VMEM((rows // 128, 128), I32), pltpu.SemaphoreType.DMA((2,))],
+        scratch_shapes=[pltpu.VMEM((rows // 128, 128), I32), pltpu.SemaphoreType.DMA((3,))],
         compiler_params=SMALL,
         name="window_sums",
     )(pltpu.with_memory_space_constraint(ids, pltpu.HBM), pltpu.with_memory_space_constraint(x, pltpu.HBM))

time: 29.6 us -> 29.5 us (level)
  no operation moved by 1% of the time
where the time goes in v2:
time: 29.5 us; the launch traced here: 29.4 us
  Pallas kernels  10.1 us (34%)
  starting transfers between devices  9.25 us (31%)
  waiting for transfers between devices  9.21 us (31%)
  between operations  0.68 us (2%)
    ppermute x7, starting transfers between devices, moved(): return lax.ppermute(a, BOTH, pairs)  9.25 us
    ppermute x7, waiting for transfers between devices, moved(): return lax.ppermute(a, BOTH, pairs)  9.21 us
    pallas_call x1, Pallas kernels, nearest_last(): pl.pallas_call(last_kernel, in_specs=[VMEM] * 5, out_specs=(HBM, HBM), ou...  3.03 us
    pallas_call x1, Pallas kernels, nearest_first(): pl.pallas_call(first_kernel, in_specs=[VMEM, VMEM], out_specs=VMEM, out_s...  2.4 us
    pallas_call x1, Pallas kernels, window_sums(): pl.pallas_call(sums_kernel, in_specs=[HBM, HBM], out_specs=(VMEM, VMEM, V...  2.32 us
    pallas_call x1, Pallas kernels, norms(): pl.pallas_call(norms_kernel, grid=(rows // chunk,), in_specs=[pl.BlockSpe...  1.58 us
    pallas_call x1, Pallas kernels, means(): pl.pallas_call(functools.partial(means_kernel, len(parts)), in_specs=[VME...  0.76 us
  transfers between devices with their start and end apart: 7, of which 6 were waited for; matrix products, arithmetic and copies ran while one was open for 0% of the time, Pallas kernels for 14%

profile of v2, /device:TPU:0, one launch (start us, length us, event | category | flops | bytes accessed | tf_op | source)
XLA Modules:
  0.0 29.4 jit_solution(11506155849028367273)
XLA Ops:
  0.6 2.3 %window_sums.1 = (s16[48,128]{1,0:T(8,128)(2,1)S(1)}, s16[48,128]{1,0:T(8,128)(2,1)S(1)}, bf16[8192,128]{1,0:T(8,128)(2,1)S(1)}) custom-call(s32[64,128]{1,0:T(8,128)} %bitcast.8, bf16[8192,128]{1,0:T(8,128)(2,1)} %x_hbm.1), custom_call_target="tpu_custom_call" | custom-call | tf_op jit(solution)/shard_map/window_sums/pallas_call | solution.py:99
  3.0 0.6 %collective-permute-start = (s16[48,128]{1,0:T(8,128)(2,1)S(1)}, s16[48,128]{1,0:T(8,128)(2,1)S(1)}, u32[]{:S(2)}, u32[]{:S(2)}) collective-permute-start(s16[48,128]{1,0:T(8,128)(2,1)S(1)} %get-tuple-element.8), channel_id=1, source_target_pairs={{0,1},{1,0},{2,3},{3,2},{4,5},{5,4},{6,7},{7,6},{8,9},{9,8},{10,11... | collective-permute-start | bytes 36872 | tf_op jit(solution)/shard_map/ppermute | solution.py:294
  3.5 0.8 %collective-permute-done = s16[48,128]{1,0:T(8,128)(2,1)S(1)} collective-permute-done((s16[48,128]{1,0:T(8,128)(2,1)S(1)}, s16[48,128]{1,0:T(8,128)(2,1)S(1)}, u32[]{:S(2)}, u32[]{:S(2)}) %collective-permute-start) | collective-permute-done | bytes 12320 | tf_op jit(solution)/shard_map/ppermute | solution.py:294
  4.4 3.8 %collective-permute-start.1 = (s16[80,128]{1,0:T(8,128)(2,1)S(1)}, s16[80,128]{1,0:T(8,128)(2,1)S(1)}, u32[]{:S(2)}, u32[]{:S(2)}) collective-permute-start(s16[80,128]{1,0:T(8,128)(2,1)S(1)} %get-tuple-element.17), channel_id=1, source_target_pairs={{0,5},{1,4},{2,7},{3,6},{4,1},{5,0},{6,3},{7,2},{8,13},{9,12},{10,... | collective-permute-start | bytes 61448 | tf_op jit(solution)/shard_map/ppermute | solution.py:294
  8.1 1.5 %collective-permute-done.1 = s16[80,128]{1,0:T(8,128)(2,1)S(1)} collective-permute-done((s16[80,128]{1,0:T(8,128)(2,1)S(1)}, s16[80,128]{1,0:T(8,128)(2,1)S(1)}, u32[]{:S(2)}, u32[]{:S(2)}) %collective-permute-start.1) | collective-permute-done | bytes 20512 | tf_op jit(solution)/shard_map/ppermute | solution.py:294
  9.6 1.6 %collective-permute-start.2 = (s16[160,128]{1,0:T(8,128)(2,1)S(1)}, s16[160,128]{1,0:T(8,128)(2,1)S(1)}, u32[]{:S(2)}, u32[]{:S(2)}) collective-permute-start(s16[160,128]{1,0:T(8,128)(2,1)S(1)} %bitcast.7), channel_id=1, source_target_pairs={{0,3},{1,2},{2,1},{3,0},{4,7},{5,6},{6,5},{7,4},{8,11},{9,10},{10,... | collective-permute-start | bytes 122888 | tf_op jit(solution)/shard_map/ppermute | solution.py:294
  11.2 1.8 %collective-permute-done.2 = s16[160,128]{1,0:T(8,128)(2,1)S(1)} collective-permute-done((s16[160,128]{1,0:T(8,128)(2,1)S(1)}, s16[160,128]{1,0:T(8,128)(2,1)S(1)}, u32[]{:S(2)}, u32[]{:S(2)}) %collective-permute-start.2) | collective-permute-done | bytes 40992 | tf_op jit(solution)/shard_map/ppermute | solution.py:294
  13.0 0.1 concatenate.13.refs_0_
  13.2 1.7 %collective-permute-start.5 = (s16[272,128]{1,0:T(8,128)(2,1)S(1)}, s16[272,128]{1,0:T(8,128)(2,1)S(1)}, u32[]{:S(2)}, u32[]{:S(2)}) collective-permute-start(s16[272,128]{1,0:T(8,128)(2,1)S(1)} %concatenate.13.refs_0_), channel_id=1, source_target_pairs={{0,9},{1,8},{2,11},{3,10},{4,13},{5,12},{6,15},{7,14},{8,1},{9,0},... | collective-permute-start | bytes 208904 | tf_op jit(solution)/shard_map/ppermute | solution.py:294
  14.8 1.5 %collective-permute-start.4 = (s16[272,128]{1,0:T(8,128)(2,1)S(1)}, s16[272,128]{1,0:T(8,128)(2,1)S(1)}, u32[]{:S(2)}, u32[]{:S(2)}) collective-permute-start(s16[272,128]{1,0:T(8,128)(2,1)S(1)} %concatenate.13.refs_0_), channel_id=1, source_target_pairs={{0,17},{1,16},{2,19},{3,18},{4,21},{5,20},{6,23},{7,22},{8,25},{9,... | collective-permute-start | bytes 208904 | tf_op jit(solution)/shard_map/ppermute | solution.py:294
  16.3 0.1 collective-permute-start.3
  16.4 0.8 %collective-permute-done.5.refs_3_ = s16[272,128]{1,0:T(8,128)(2,1)S(1)} collective-permute-done((s16[272,128]{1,0:T(8,128)(2,1)S(1)}, s16[272,128]{1,0:T(8,128)(2,1)S(1)}, u32[]{:S(2)}, u32[]{:S(2)}) %collective-permute-start.5) | collective-permute-done | bytes 69664 | tf_op jit(solution)/shard_map/ppermute | solution.py:294
  17.3 2.6 %collective-permute-done.4.refs_2_ = s16[272,128]{1,0:T(8,128)(2,1)S(1)} collective-permute-done((s16[272,128]{1,0:T(8,128)(2,1)S(1)}, s16[272,128]{1,0:T(8,128)(2,1)S(1)}, u32[]{:S(2)}, u32[]{:S(2)}) %collective-permute-start.4) | collective-permute-done | bytes 69664 | tf_op jit(solution)/shard_map/ppermute | solution.py:294
  19.9 1.6 %collective-permute-done.3.refs_1_ = s16[272,128]{1,0:T(8,128)(2,1)S(1)} collective-permute-done((s16[272,128]{1,0:T(8,128)(2,1)S(1)}, s16[272,128]{1,0:T(8,128)(2,1)S(1)}, u32[]{:S(2)}, u32[]{:S(2)}) %collective-permute-start.3) | collective-permute-done | bytes 69664 | tf_op jit(solution)/shard_map/ppermute | solution.py:294
  21.5 0.8 %means.1.table_ref.mine_ref = bf16[512,256]{1,0:T(8,128)(2,1)S(1)} custom-call(s16[272,128]{1,0:T(8,128)(2,1)S(1)} %concatenate.13.refs_0_, s16[272,128]{1,0:T(8,128)(2,1)S(1)} %collective-permute-done.3.refs_1_, s16[272,128]{1,0:T(8,128)(2,1)S(1)} %collective-permute-done.4.refs_2_, s16[272,128]{1,0:T(8,128)(2,1)S(1)} %collective-permute-done.5.refs_3_), custom_call_target="tpu_custom_call" | custom-call | tf_op jit(solution)/shard_map/means/pallas_call | solution.py:203
  22.3 0.1 collective-permute-start.6
  22.4 1.6 %norms.1.norm_ref = f32[64,128]{1,0:T(8,128)S(1)} custom-call(bf16[8192,128]{1,0:T(8,128)(2,1)S(1)} %get-tuple-element.9.x_ref), custom_call_target="tpu_custom_call" | custom-call | flops 2097152 | bytes 2097152 | tf_op jit(solution)/shard_map/norms/pallas_call | solution.py:126
  23.9 2.4 %nearest_first.1.near_ref = f32[64,128]{1,0:T(8,128)S(1)} custom-call(bf16[512,256]{1,0:T(8,128)(2,1)S(1)} %means.1.table_ref.mine_ref, bf16[8192,128]{1,0:T(8,128)(2,1)S(1)} %get-tuple-element.9.x_ref), custom_call_target="tpu_custom_call" | custom-call | flops 2147483648 | bytes 2097152 | tf_op jit(solution)/shard_map/nearest_first/pallas_call | solution.py:264
  26.3 0.0 collective-permute-done.6.table_ref
  26.4 3.0 %nearest_last.1 = (bf16[128,128]{1,0:T(8,128)(2,1)}, f32[64,128]{1,0:T(8,128)}) custom-call(bf16[512,256]{1,0:T(8,128)(2,1)S(1)} %collective-permute-done.6.table_ref, bf16[8192,128]{1,0:T(8,128)(2,1)S(1)} %get-tuple-element.9.x_ref, bf16[512,256]{1,0:T(8,128)(2,1)S(1)} %means.1.table_ref.mine_ref, f32[64,128]{1,0:T(8,128)S(1)} %nearest_first.1.near_ref, ...), custom_call_target="tpu_custom_call" | custom-call | flops 2147483648 | bytes 2097152 | tf_op jit(solution)/shard_map/nearest_last/pallas_call | solution.py:279
  (11 shorter events, 0.0 us)
Async XLA Ops:
  3.0 1.4 %collective-permute-start = (s16[48,128]{1,0:T(8,128)(2,1)S(1)}, s16[48,128]{1,0:T(8,128)(2,1)S(1)}, u32[]{:S(2)}, u32[]{:S(2)}) collective-permute-start(s16[48,128]{1,0:T(8,128)(2,1)S(1)} %get-tuple-element.8), channel_id=1, source_target_pairs={{0,1},{1,0},{2,3},{3,2},{4,5},{5,4},{6,7},{7,6},{8,9},{9,8},{10,11... | collective-permute-start | bytes 36872 | tf_op jit(solution)/shard_map/ppermute | solution.py:294
  4.4 5.2 %collective-permute-start.1 = (s16[80,128]{1,0:T(8,128)(2,1)S(1)}, s16[80,128]{1,0:T(8,128)(2,1)S(1)}, u32[]{:S(2)}, u32[]{:S(2)}) collective-permute-start(s16[80,128]{1,0:T(8,128)(2,1)S(1)} %get-tuple-element.17), channel_id=1, source_target_pairs={{0,5},{1,4},{2,7},{3,6},{4,1},{5,0},{6,3},{7,2},{8,13},{9,12},{10,... | collective-permute-start | bytes 61448 | tf_op jit(solution)/shard_map/ppermute | solution.py:294
  9.6 3.4 %collective-permute-start.2 = (s16[160,128]{1,0:T(8,128)(2,1)S(1)}, s16[160,128]{1,0:T(8,128)(2,1)S(1)}, u32[]{:S(2)}, u32[]{:S(2)}) collective-permute-start(s16[160,128]{1,0:T(8,128)(2,1)S(1)} %bitcast.7), channel_id=1, source_target_pairs={{0,3},{1,2},{2,1},{3,0},{4,7},{5,6},{6,5},{7,4},{8,11},{9,10},{10,... | collective-permute-start | bytes 122888 | tf_op jit(solution)/shard_map/ppermute | solution.py:294
  13.2 4.1 %collective-permute-start.5 = (s16[272,128]{1,0:T(8,128)(2,1)S(1)}, s16[272,128]{1,0:T(8,128)(2,1)S(1)}, u32[]{:S(2)}, u32[]{:S(2)}) collective-permute-start(s16[272,128]{1,0:T(8,128)(2,1)S(1)} %concatenate.13.refs_0_), channel_id=1, source_target_pairs={{0,9},{1,8},{2,11},{3,10},{4,13},{5,12},{6,15},{7,14},{8,1},{9,0},... | collective-permute-start | bytes 208904 | tf_op jit(solution)/shard_map/ppermute | solution.py:294
  14.8 5.0 %collective-permute-start.4 = (s16[272,128]{1,0:T(8,128)(2,1)S(1)}, s16[272,128]{1,0:T(8,128)(2,1)S(1)}, u32[]{:S(2)}, u32[]{:S(2)}) collective-permute-start(s16[272,128]{1,0:T(8,128)(2,1)S(1)} %concatenate.13.refs_0_), channel_id=1, source_target_pairs={{0,17},{1,16},{2,19},{3,18},{4,21},{5,20},{6,23},{7,22},{8,25},{9,... | collective-permute-start | bytes 208904 | tf_op jit(solution)/shard_map/ppermute | solution.py:294
  16.3 5.2 %collective-permute-start.3 = (s16[272,128]{1,0:T(8,128)(2,1)S(1)}, s16[272,128]{1,0:T(8,128)(2,1)S(1)}, u32[]{:S(2)}, u32[]{:S(2)}) collective-permute-start(s16[272,128]{1,0:T(8,128)(2,1)S(1)} %concatenate.13.refs_0_), channel_id=1, source_target_pairs={{0,24},{1,25},{2,26},{3,27},{4,28},{5,29},{6,30},{7,31},{8,16},{9,... | collective-permute-start | bytes 208904 | tf_op jit(solution)/shard_map/ppermute | solution.py:294
  22.3 4.1 %collective-permute-start.6 = (bf16[512,256]{1,0:T(8,128)(2,1)S(1)}, bf16[512,256]{1,0:T(8,128)(2,1)S(1)}, u32[]{:S(2)}, u32[]{:S(2)}) collective-permute-start(bf16[512,256]{1,0:T(8,128)(2,1)S(1)} %means.1.table_ref.mine_ref), channel_id=1, source_target_pairs={{0,1},{1,0},{2,3},{3,2},{4,5},{5,4},{6,7},{7,6},{8,9},{9,8},{10,11... | collective-permute-start | bytes 786440 | tf_op jit(solution)/shard_map/ppermute | solution.py:294
